TPU v7x, 32 devices: a whole 2x2x4 slice. The times are simulated.
32 devices in a mesh: segment: 4 (over z), ctx: 4 (over y, x), tp: 2 (over core).
Axes of the slice: x: 2, y: 2, z: 4, core: 2. Of those that a mesh axis runs over, the one named last changes fastest.
Arguments:
- queries: bfloat16 [4, 512, 8, 640], P('segment', 'ctx', 'tp'), may hold values from -200 to 200
- pairs: bfloat16 [4, 512, 8, 256], P('segment', 'ctx', 'tp'), may hold values from -6 to 6
- out_proj: bfloat16 [4, 8, 640, 5120], P('segment', 'tp'), may hold values from -0.625 to 0.625
- lengths: int32 [4, 4], replicated, may hold values from 1 to 256, 512 in all within a row
Outputs:
- scored: bfloat16 [4, 512, 5120], P('segment', 'ctx', 'tp')
Inputs may be any that keep to these rules, and one draw needn't show every extreme that they name: `lengths`: each row sums to 512; its largest length is exactly 256.
All inputs are finite; a program needn't handle non-finite values.
Results may differ from a plain program's by a relative error of at most 0.014.
Values may be sent and summed in bfloat16 or wider, within the bound.
A program may use at most 64 MiB of HBM per device.

v0:
```python
import math
import jax
import jax.numpy as jnp
from jax import lax
from jax.sharding import PartitionSpec as P


def from_behind(value, axis, by):
    size = lax.axis_size(axis)
    return lax.ppermute(value, axis, [(i, (i + by) % size) for i in range(size)])


def rollout_ids(positions, row_lengths):
    row_ends = jnp.cumsum(row_lengths)
    return jnp.sum((positions[:, None] >= row_ends[None, :]).astype(jnp.int32), axis=1)


def attend(query_shard, pair_shard, row_lengths):
    rows_here = query_shard.shape[1]
    local_heads = pair_shard.shape[2]
    head_dim = pair_shard.shape[3] // 2
    group_size = query_shard.shape[3] // head_dim
    first_pos = lax.axis_index("ctx") * rows_here
    query_pos = first_pos + jnp.arange(rows_here, dtype=jnp.int32)
    query_rollout = rollout_ids(query_pos, row_lengths)
    query_heads = query_shard[0].reshape(rows_here, local_heads, group_size, head_dim)
    score_scale = 1.0 / math.sqrt(head_dim)

    def update(state_in, key_block, key_begin):
        running_max, denom, accum = state_in
        block_len = key_block.shape[0]
        key_pos = key_begin + jnp.arange(block_len, dtype=jnp.int32)
        key_rollout = rollout_ids(key_pos, row_lengths)
        visible = (query_rollout[:, None] == key_rollout[None, :]) & (
            key_pos[None, :] <= query_pos[:, None]
        )
        scores = (
            jnp.einsum(
                "rhgd,khd->hgrk",
                query_heads,
                key_block[:, :, :head_dim],
                preferred_element_type=jnp.float32,
            )
            * score_scale
        )
        scores = jnp.where(visible, scores, -1e30)
        new_max = jnp.maximum(running_max, jnp.max(scores, axis=-1))
        rescale = jnp.exp(running_max - new_max)
        weights = jnp.where(visible, jnp.exp(scores - new_max[..., None]), 0.0)
        denom = denom * rescale + jnp.sum(weights, axis=-1)
        added = jnp.einsum(
            "hgrk,khd->hgrd",
            weights.astype(jnp.bfloat16),
            key_block[:, :, head_dim:],
            preferred_element_type=jnp.float32,
        )
        accum = accum * rescale[..., None] + added
        return (new_max, denom, accum)

    starting = (
        jnp.full((local_heads, group_size, rows_here), -1e30, jnp.float32),
        jnp.zeros((local_heads, group_size, rows_here), jnp.float32),
        jnp.zeros((local_heads, group_size, rows_here, head_dim), jnp.float32),
    )
    shards = lax.all_gather(pair_shard[0], "ctx", axis=0, tiled=True)
    shard_rows = shards.shape[0]
    block_len = math.gcd(shard_rows, 512)

    def one_step(step_index, inner):
        key_block = lax.dynamic_slice_in_dim(shards, step_index * block_len, block_len, 0)
        return update(inner, key_block, step_index * block_len)

    running_max, denom, accum = lax.fori_loop(0, shard_rows // block_len, one_step, starting)
    outputs = accum / denom[..., None]
    outputs = jnp.transpose(outputs, (2, 0, 1, 3)).reshape(
        1, rows_here, local_heads, group_size * head_dim
    )
    return outputs.astype(jnp.bfloat16)


def local(queries, pairs, out_proj, lengths):
    section = lax.axis_index("segment")
    own_result = attend(queries, pairs, lengths[section])
    attended = from_behind(own_result, "segment", -1)
    rows_here = attended.shape[1]
    partial_sum = jnp.dot(
        attended.reshape(rows_here, -1),
        out_proj[0].reshape(-1, out_proj.shape[3]),
        preferred_element_type=jnp.float32,
    )
    shares = lax.psum_scatter(
        partial_sum.astype(jnp.bfloat16), "tp", scatter_dimension=1, tiled=True
    )
    return shares.reshape(1, rows_here, -1)


def solution(mesh):
    return jax.shard_map(
        local,
        mesh=mesh,
        in_specs=(
            P("segment", "ctx", "tp", None),
            P("segment", "ctx", "tp", None),
            P("segment", "tp", None, None),
            P(),
        ),
        out_specs=P("segment", "ctx", "tp"),
        check_vma=False,
    )
```

profile of v0, /device:TPU:0, one launch (start us, length us, event | category | flops | bytes accessed | tf_op | source)
XLA Modules:
  0.0 89.1 jit_solution(15405422814970957084)
XLA Ops:
  6.5 0.0 copy-start
  6.5 0.0 all-gather.3.cloned.1.call-start
  6.5 1.7 %copy.16 = bf16[1,128,4,256]{3,1,2,0:T(8,128)(2,1)} copy(bf16[1,128,4,256]{3,2,1,0:T(4,128)(2,1)} %param.5) | data formatting | bytes 524288 | tf_op args[1]
  8.2 0.0 all-gather.3.cloned.1.call-update
  8.3 0.0 reduce-scatter.2.cloned.1.call-start
  8.3 0.0 copy-done
  8.3 0.2 reduce-window.8
  8.5 1.6 %copy.17 = bf16[1,128,4,640]{1,3,2,0:T(8,128)(2,1)S(1)} copy(bf16[1,128,4,640]{3,2,1,0:T(4,128)(2,1)} %param.4) | data formatting | bytes 1310720 | tf_op args[0]
  10.1 0.1 convert_reduce_fusion
  10.2 0.1 convert_reduce_fusion.1
  10.3 0.1 fusion.24
  10.4 28.0 %all-gather.3.cloned.1.call-done = bf16[1,512,4,256]{3,1,2,0:T(8,128)(2,1)} async-done(((bf16[1,128,4,256]{3,1,2,0:T(8,128)(2,1)}), bf16[1,512,4,256]{3,1,2,0:T(8,128)(2,1)}) %all-gather.3.cloned.1.call-update) | async-done | bytes 1048592 | tf_op jit(solution)/shard_map/all_gather | solution.py:65
  38.4 0.0 copy-start.1
  38.4 2.0 %fusion.8 = (f32[4,5,128]{2,1,0:T(8,128)S(1)}, f32[4,512,128,5]{2,1,3,0:T(8,128)S(1)}) fusion(pred[128,512]{0,1:T(8,128)(4,1)S(1)} %fusion.24, bf16[128,4,5,128]{0,3,2,1:T(8,128)(2,1)S(1)} %bitcast.63, bf16[512,4,256]{2,0,1:T(8,128)(2,1)} %bitcast.65), kind=kOutput, calls=%fused_computation.6 | convolution fusion | flops 339473920 | bytes 6498304 | tf_op jit(solution)/shard_map/while/body/eval_jaxpr/rhgd,khd->hgrk/dot_general | solution.py:38
  40.5 1.3 %fusion.9 = f32[4,5,128]{2,1,0:T(8,128)S(1)} fusion(f32[4,512,128,5]{2,1,3,0:T(8,128)S(1)} %get-tuple-element.26, f32[4,5,128]{2,1,0:T(8,128)S(1)} %get-tuple-element.24, pred[128,512]{0,1:T(8,128)(4,1)S(1)} %fusion.24), kind=kLoop, calls=%fused_computation.7 | loop fusion | flops 6551040 | bytes 5328896 | tf_op jit(solution)/shard_map/while/body/eval_jaxpr/reduce_sum | solution.py:50
  41.8 0.0 copy-done.1
  41.8 1.5 %divide_convert_fusion = bf16[128,4,5,128]{0,3,2,1:T(8,128)(2,1)S(1)} fusion(f32[4,512,128,5]{2,1,3,0:T(8,128)S(1)} %get-tuple-element.26, f32[4,5,128]{2,1,0:T(8,128)S(1)} %get-tuple-element.24, pred[128,512]{0,1:T(8,128)(4,1)S(1)} %fusion.24, f32[128,4,5]{0,2,1:T(8,128)S(1)} %bitcast_add_fusion, f32[128,4,5]{0,2,1:T(8,128)S(1)} %get-tuple-element.23, ...), kind=kOutput, calls=%fused_computation.13 | convolution fusion | flops 343080960 | bytes 6537216 | tf_op jit(solution)/shard_map/while/body/eval_jaxpr/hgrk,khd->hgrd/dot_general | solution.py:51
  43.3 0.3 copy.21
  43.6 3.4 %collective-permute-start = (bf16[1,128,4,640]{3,1,2,0:T(8,128)(2,1)S(1)}, bf16[1,128,4,640]{3,1,2,0:T(8,128)(2,1)S(1)}, u32[]{:S(2)}, u32[]{:S(2)}) collective-permute-start(bf16[1,128,4,640]{3,1,2,0:T(8,128)(2,1)S(1)} %copy.21), channel_id=1, source_target_pairs={{0,24},{8,0},{16,8},{24,16},{1,25},{9,1},{17,9},{25,17},{2,26},{10... | collective-permute-start | bytes 1966088 | tf_op jit(solution)/shard_map/ppermute | solution.py:10
  47.0 13.8 %collective-permute-done = bf16[1,128,4,640]{3,1,2,0:T(8,128)(2,1)S(1)} collective-permute-done((bf16[1,128,4,640]{3,1,2,0:T(8,128)(2,1)S(1)}, bf16[1,128,4,640]{3,1,2,0:T(8,128)(2,1)S(1)}, u32[]{:S(2)}, u32[]{:S(2)}) %collective-permute-start) | collective-permute-done | bytes 655392 | tf_op jit(solution)/shard_map/ppermute | solution.py:10
  60.8 11.7 %fusion.5 = bf16[128,5120]{1,0:T(8,128)(2,1)} fusion(bf16[1,4,640,5120]{3,2,1,0:T(8,128)(2,1)} %param.6, bf16[1,128,4,640]{3,1,2,0:T(8,128)(2,1)S(1)} %collective-permute-done), kind=kOutput, calls=%fused_computation.3 | convolution fusion | flops 3356098560 | bytes 28180480 | tf_op jit(solution)/shard_map/dot_general | solution.py:86
  72.5 0.0 reduce-scatter.2.cloned.1.call-update
  72.6 9.7 %reduce-scatter.2.cloned.1.call-done = bf16[128,2560]{1,0:T(8,128)(2,1)} async-done(((bf16[128,5120]{1,0:T(8,128)(2,1)}), bf16[128,2560]{1,0:T(8,128)(2,1)}) %reduce-scatter.2.cloned.1.call-update) | async-done | bytes 655376 | tf_op jit(solution)/shard_map/reduce_scatter | solution.py:91
  (4 shorter events, 0.0 us)
Async XLA Ops:
  6.5 1.8 %copy-start = (s32[4,4]{1,0:T(4,128)S(1)}, s32[4,4]{1,0:T(4,128)}, u32[]{:S(2)}) copy-start(s32[4,4]{1,0:T(4,128)} %param.7) | copy-start | bytes 196
  6.5 31.9 %all-gather.3.cloned.1.call-start = ((), (), s32[]{:S(2)}) async-start(), calls=%async_computation.2 | async-start | bytes 1310720 | tf_op jit(solution)/shard_map/all_gather | solution.py:65
  8.3 74.0 %reduce-scatter.2.cloned.1.call-start = ((), (), s32[]{:S(2)}) async-start(), calls=%async_computation.1 | async-start | bytes 1966080 | tf_op jit(solution)/shard_map/reduce_scatter | solution.py:91
  38.4 3.3 %copy-start.1 = (bf16[1,512,4,256]{3,1,2,0:T(8,128)(2,1)S(1)}, bf16[1,512,4,256]{3,1,2,0:T(8,128)(2,1)}, u32[]{:S(2)}) copy-start(bf16[1,512,4,256]{3,1,2,0:T(8,128)(2,1)} %all-gather.3.cloned.1.call-done) | copy-start | bytes 3145732
  43.6 17.2 %collective-permute-start = (bf16[1,128,4,640]{3,1,2,0:T(8,128)(2,1)S(1)}, bf16[1,128,4,640]{3,1,2,0:T(8,128)(2,1)S(1)}, u32[]{:S(2)}, u32[]{:S(2)}) collective-permute-start(bf16[1,128,4,640]{3,1,2,0:T(8,128)(2,1)S(1)} %copy.21), channel_id=1, source_target_pairs={{0,24},{8,0},{16,8},{24,16},{1,25},{9,1},{17,9},{25,17},{2,26},{10... | collective-permute-start | bytes 1966088 | tf_op jit(solution)/shard_map/ppermute | solution.py:10
Sparse Core Ops, SparseCore 0:
  9.2 29.2 all-gather.2
  72.7 9.5 reduce-scatter.1
where the time goes:
time: 89.3 us; the launch traced here: 89.1 us
  waiting for transfers between devices  51.6 us (58%)
  matrix products  15.2 us (17%)
  between operations  13.5 us (15%)
  local copies, waits for them, and re-layouts  3.62 us (4%)
  starting transfers between devices  3.43 us (4%)
  other arithmetic  1.76 us (2%)
    all_gather x1, waiting for transfers between devices, attend(): shards = lax.all_gather(pair_shard[0], 'ctx', axis=0, tiled=True)  28 us
    ppermute x1, waiting for transfers between devices, from_behind(): lax.ppermute(value, axis, [(i, (i + by) % size) for i in range(size)])  13.8 us
    dot_general x1, matrix products, local(): jnp.dot(attended.reshape(rows_here, -1), out_proj[0].reshape(-1, out_proj...  11.7 us
    reduce_scatter x1, waiting for transfers between devices, local(): lax.psum_scatter(partial_sum.astype(jnp.bfloat16), 'tp', scatter_dimensio...  9.74 us
    ppermute x1, starting transfers between devices, from_behind(): lax.ppermute(value, axis, [(i, (i + by) % size) for i in range(size)])  3.38 us
    unnamed x6, local copies, waits for them, and re-layouts  3.29 us
    dot_general x1, matrix products, update(): jnp.einsum('rhgd,khd->hgrk', query_heads, key_block[:, :, :head_dim], pre...  2.02 us
  transfers between devices with their start and end apart: 3, of which 3 were waited for; matrix products, arithmetic and copies ran while one was open for 2% of the time, Pallas kernels for 0%

commit v1 on v0

--- a/solution.py
+++ b/solution.py
@@ -3,6 +3,22 @@
 import jax.numpy as jnp
 from jax import lax
 from jax.sharding import PartitionSpec as P
+
+
+def gather_around(x, axis, dim):
+    ways, here, lap = (lax.axis_size(axis), lax.axis_index(axis), x.shape[dim])
+    shape = [n * ways if d == dim else n for d, n in enumerate(x.shape)]
+    full = lax.dynamic_update_slice_in_dim(jnp.zeros(shape, x.dtype), x, here * lap, axis=dim)
+    going_up = going_down = x
+    for far in range(1, ways // 2 + 1):
+        going_up = lax.ppermute(going_up, axis, [(d, (d + 1) % ways) for d in range(ways)])
+        full = lax.dynamic_update_slice_in_dim(full, going_up, (here - far) % ways * lap, axis=dim)
+        if 2 * far < ways:
+            going_down = lax.ppermute(going_down, axis, [(d, (d - 1) % ways) for d in range(ways)])
+            full = lax.dynamic_update_slice_in_dim(
+                full, going_down, (here + far) % ways * lap, axis=dim
+            )
+    return full
 
 
 def from_behind(value, axis, by):
@@ -62,7 +78,7 @@
         jnp.zeros((local_heads, group_size, rows_here), jnp.float32),
         jnp.zeros((local_heads, group_size, rows_here, head_dim), jnp.float32),
     )
-    shards = lax.all_gather(pair_shard[0], "ctx", axis=0, tiled=True)
+    shards = gather_around(pair_shard[0], "ctx", 0)
     shard_rows = shards.shape[0]
     block_len = math.gcd(shard_rows, 512)
 

time: 89.3 us -> 78.7 us (0.88)
  waiting for transfers between devices: 51.6 us -> 36.1 us
  starting transfers between devices: 3.43 us -> 8.95 us
  matrix products: 15.2 us -> 14.1 us
    all_gather x1 -> x0, waiting for transfers between devices: 28 us -> none  [attend(): shards = lax.all_gather(pair_shard[0], 'ctx', axis=0, tiled=True)]
    ppermute x0 -> x3, waiting for transfers between devices: none -> 13.1 us  [the longest x2 9.87 us: gather_around(): lax.ppermute(going_up, axis, [(d, (d + 1) % ways) for d in range(ways)])]
    ppermute x0 -> x3, starting transfers between devices: none -> 5.1 us  [the longest x2 4.08 us: gather_around(): lax.ppermute(going_up, axis, [(d, (d + 1) % ways) for d in range(ways)])]
    dot_general x1, matrix products: 2.02 us -> 0.92 us  [update(): jnp.einsum('rhgd,khd->hgrk', query_heads, key_block[:, :, :head_dim], pre...]
    dynamic_update_slice x0 -> x4, local copies, waits for them, and re-layouts: none -> 1.05 us  [the longest x1 0.99 us: gather_around(): lax.dynamic_update_slice_in_dim(jnp.zeros(shape, x.dtype), x, here * lap,...]
    unnamed x6 -> x4, local copies, waits for them, and re-layouts: 3.29 us -> 2.6 us
  transfers between devices with their start and end apart: 3 -> 5, of which waited for: 3 -> 5; matrix products, arithmetic and copies ran while one was open for 2% -> 4% of each run, Pallas kernels for 0% -> 0%
where the time goes in v1:
time: 78.7 us; the launch traced here: 78.5 us
  waiting for transfers between devices  36.1 us (46%)
  matrix products  14.1 us (18%)
  between operations  13.5 us (17%)
  starting transfers between devices  8.95 us (11%)
  local copies, waits for them, and re-layouts  4.05 us (5%)
  other arithmetic  1.76 us (2%)
    ppermute x1, waiting for transfers between devices, from_behind(): lax.ppermute(value, axis, [(i, (i + by) % size) for i in range(size)])  13.1 us
    dot_general x1, matrix products, local(): jnp.dot(attended.reshape(rows_here, -1), out_proj[0].reshape(-1, out_proj...  11.7 us
    ppermute x2, waiting for transfers between devices, gather_around(): lax.ppermute(going_up, axis, [(d, (d + 1) % ways) for d in range(ways)])  9.87 us
    reduce_scatter x1, waiting for transfers between devices, local(): lax.psum_scatter(partial_sum.astype(jnp.bfloat16), 'tp', scatter_dimensio...  9.82 us
    ppermute x2, starting transfers between devices, gather_around(): lax.ppermute(going_up, axis, [(d, (d + 1) % ways) for d in range(ways)])  4.08 us
    ppermute x1, starting transfers between devices, from_behind(): lax.ppermute(value, axis, [(i, (i + by) % size) for i in range(size)])  3.85 us
    ppermute x1, waiting for transfers between devices, gather_around(): lax.ppermute(going_down, axis, [(d, (d - 1) % ways) for d in range(ways)])  3.23 us
    unnamed x4, local copies, waits for them, and re-layouts  2.6 us
  transfers between devices with their start and end apart: 5, of which 5 were waited for; matrix products, arithmetic and copies ran while one was open for 4% of the time, Pallas kernels for 0%

profile of v1, /device:TPU:0, one launch (start us, length us, event | category | flops | bytes accessed | tf_op | source)
XLA Modules:
  0.0 78.5 jit_solution(12918237970220569508)
XLA Ops:
  6.5 0.0 copy-start
  6.5 0.0 reduce-scatter.2.cloned.1.call-start
  6.5 1.0 %copy.31 = bf16[1,128,4,256]{3,1,2,0:T(8,128)(2,1)S(1)} copy(bf16[1,128,4,256]{3,2,1,0:T(4,128)(2,1)} %param.5) | data formatting | bytes 524288 | tf_op args[1]
  7.5 3.0 %collective-permute-start = (bf16[128,4,256]{2,0,1:T(8,128)(2,1)S(1)}, bf16[128,4,256]{2,0,1:T(8,128)(2,1)S(1)}, u32[]{:S(2)}, u32[]{:S(2)}) collective-permute-start(bf16[128,4,256]{2,0,1:T(8,128)(2,1)S(1)} %bitcast.69), channel_id=1, source_target_pairs={{0,2},{2,4},{4,6},{6,0},{1,3},{3,5},{5,7},{7,1},{8,10},{10,12},{12... | collective-permute-start | bytes 786440 | tf_op jit(solution)/shard_map/ppermute | solution.py:14
  10.6 1.0 %collective-permute-start.1 = (bf16[128,4,256]{2,0,1:T(8,128)(2,1)S(1)}, bf16[128,4,256]{2,0,1:T(8,128)(2,1)S(1)}, u32[]{:S(2)}, u32[]{:S(2)}) collective-permute-start(bf16[128,4,256]{2,0,1:T(8,128)(2,1)S(1)} %bitcast.70), channel_id=1, source_target_pairs={{0,6},{2,0},{4,2},{6,4},{1,7},{3,1},{5,3},{7,5},{8,14},{10,8},{12,... | collective-permute-start | bytes 786440 | tf_op jit(solution)/shard_map/ppermute | solution.py:17
  11.6 0.0 copy-done
  11.6 0.2 reduce-window.8
  11.8 0.1 convert_reduce_fusion.1
  11.9 0.1 convert_reduce_fusion
  11.9 0.1 broadcast_in_dim.47
  12.0 1.0 %constant_dynamic-update-slice_fusion.3 = bf16[512,4,256]{2,0,1:T(8,128)(2,1)S(1)} fusion(bf16[512,4,256]{2,0,1:T(8,128)(2,1)S(1)} %broadcast_in_dim.47, s32[]{:T(128)S(6)} %select_n.42, bf16[1,128,4,256]{3,2,1,0:T(4,128)(2,1)} %param.5), kind=kLoop, calls=%fused_computation.30 | loop fusion | bytes 524292 | tf_op jit(solution)/shard_map/dynamic_update_slice | solution.py:11
  13.0 5.7 %collective-permute-done = bf16[128,4,256]{2,0,1:T(8,128)(2,1)S(1)} collective-permute-done((bf16[128,4,256]{2,0,1:T(8,128)(2,1)S(1)}, bf16[128,4,256]{2,0,1:T(8,128)(2,1)S(1)}, u32[]{:S(2)}, u32[]{:S(2)}) %collective-permute-start) | collective-permute-done | bytes 262176 | tf_op jit(solution)/shard_map/ppermute | solution.py:14
  18.7 1.1 %collective-permute-start.2 = (bf16[128,4,256]{2,0,1:T(8,128)(2,1)S(1)}, bf16[128,4,256]{2,0,1:T(8,128)(2,1)S(1)}, u32[]{:S(2)}, u32[]{:S(2)}) collective-permute-start(bf16[128,4,256]{2,0,1:T(8,128)(2,1)S(1)} %collective-permute-done), channel_id=1, source_target_pairs={{0,2},{2,4},{4,6},{6,0},{1,3},{3,5},{5,7},{7,1},{8,10},{10,12},{12... | collective-permute-start | bytes 786440 | tf_op jit(solution)/shard_map/ppermute | solution.py:14
  19.7 0.1 fusion.24
  19.9 1.6 %copy.17 = bf16[1,128,4,640]{1,3,2,0:T(8,128)(2,1)S(1)} copy(bf16[1,128,4,640]{3,2,1,0:T(4,128)(2,1)} %param.4) | data formatting | bytes 1310720 | tf_op args[0]
  21.6 3.2 %collective-permute-done.1 = bf16[128,4,256]{2,0,1:T(8,128)(2,1)S(1)} collective-permute-done((bf16[128,4,256]{2,0,1:T(8,128)(2,1)S(1)}, bf16[128,4,256]{2,0,1:T(8,128)(2,1)S(1)}, u32[]{:S(2)}, u32[]{:S(2)}) %collective-permute-start.1) | collective-permute-done | bytes 262176 | tf_op jit(solution)/shard_map/ppermute | solution.py:17
  24.8 4.2 %collective-permute-done.2 = bf16[128,4,256]{2,0,1:T(8,128)(2,1)S(1)} collective-permute-done((bf16[128,4,256]{2,0,1:T(8,128)(2,1)S(1)}, bf16[128,4,256]{2,0,1:T(8,128)(2,1)S(1)}, u32[]{:S(2)}, u32[]{:S(2)}) %collective-permute-start.2) | collective-permute-done | bytes 262176 | tf_op jit(solution)/shard_map/ppermute | solution.py:14
  29.1 0.9 %fusion.8 = (f32[4,5,128]{2,1,0:T(8,128)S(1)}, f32[4,512,128,5]{2,1,3,0:T(8,128)S(1)}) fusion(pred[128,512]{0,1:T(8,128)(4,1)S(1)} %fusion.24, bf16[128,4,5,128]{0,3,2,1:T(8,128)(2,1)S(1)} %bitcast.67, bf16[512,4,256]{2,0,1:T(8,128)(2,1)S(1)} %constant_dynamic-update-slice_fusion), kind=kOutput, calls=%fused_computation.6 | convolution fusion | flops 339473920 | bytes 6498304 | tf_op jit(solution)/shard_map/while/body/eval_jaxpr/rhgd,khd->hgrk/dot_general | solution.py:54
  30.0 1.3 %fusion.9 = f32[4,5,128]{2,1,0:T(8,128)S(1)} fusion(f32[4,512,128,5]{2,1,3,0:T(8,128)S(1)} %get-tuple-element.26, f32[4,5,128]{2,1,0:T(8,128)S(1)} %get-tuple-element.24, pred[128,512]{0,1:T(8,128)(4,1)S(1)} %fusion.24), kind=kLoop, calls=%fused_computation.7 | loop fusion | flops 6551040 | bytes 5328896 | tf_op jit(solution)/shard_map/while/body/eval_jaxpr/reduce_sum | solution.py:66
  31.3 1.5 %divide_convert_fusion = bf16[128,4,5,128]{0,3,2,1:T(8,128)(2,1)S(1)} fusion(f32[4,512,128,5]{2,1,3,0:T(8,128)S(1)} %get-tuple-element.26, f32[4,5,128]{2,1,0:T(8,128)S(1)} %get-tuple-element.24, pred[128,512]{0,1:T(8,128)(4,1)S(1)} %fusion.24, f32[128,4,5]{0,2,1:T(8,128)S(1)} %bitcast_add_fusion, f32[128,4,5]{0,2,1:T(8,128)S(1)} %get-tuple-element.23, ...), kind=kOutput, calls=%fused_computation.13 | convolution fusion | flops 343080960 | bytes 6537216 | tf_op jit(solution)/shard_map/while/body/eval_jaxpr/hgrk,khd->hgrd/dot_general | solution.py:67
  32.8 0.3 copy.21
  33.1 3.8 %collective-permute-start.3 = (bf16[1,128,4,640]{3,1,2,0:T(8,128)(2,1)S(1)}, bf16[1,128,4,640]{3,1,2,0:T(8,128)(2,1)S(1)}, u32[]{:S(2)}, u32[]{:S(2)}) collective-permute-start(bf16[1,128,4,640]{3,1,2,0:T(8,128)(2,1)S(1)} %copy.21), channel_id=1, source_target_pairs={{0,24},{8,0},{16,8},{24,16},{1,25},{9,1},{17,9},{25,17},{2,26},{10... | collective-permute-start | bytes 1966088 | tf_op jit(solution)/shard_map/ppermute | solution.py:26
  37.0 13.1 %collective-permute-done.3 = bf16[1,128,4,640]{3,1,2,0:T(8,128)(2,1)S(1)} collective-permute-done((bf16[1,128,4,640]{3,1,2,0:T(8,128)(2,1)S(1)}, bf16[1,128,4,640]{3,1,2,0:T(8,128)(2,1)S(1)}, u32[]{:S(2)}, u32[]{:S(2)}) %collective-permute-start.3) | collective-permute-done | bytes 655392 | tf_op jit(solution)/shard_map/ppermute | solution.py:26
  50.1 11.7 %fusion.5 = bf16[128,5120]{1,0:T(8,128)(2,1)} fusion(bf16[1,4,640,5120]{3,2,1,0:T(8,128)(2,1)} %param.6, bf16[1,128,4,640]{3,1,2,0:T(8,128)(2,1)S(1)} %collective-permute-done.3), kind=kOutput, calls=%fused_computation.3 | convolution fusion | flops 3356098560 | bytes 28180480 | tf_op jit(solution)/shard_map/dot_general | solution.py:102
  61.8 0.0 reduce-scatter.2.cloned.1.call-update
  61.9 9.8 %reduce-scatter.2.cloned.1.call-done = bf16[128,2560]{1,0:T(8,128)(2,1)} async-done(((bf16[128,5120]{1,0:T(8,128)(2,1)}), bf16[128,2560]{1,0:T(8,128)(2,1)}) %reduce-scatter.2.cloned.1.call-update) | async-done | bytes 655376 | tf_op jit(solution)/shard_map/reduce_scatter | solution.py:107
  (7 shorter events, 0.1 us)
Async XLA Ops:
  6.5 5.0 %copy-start = (s32[4,4]{1,0:T(4,128)S(1)}, s32[4,4]{1,0:T(4,128)}, u32[]{:S(2)}) copy-start(s32[4,4]{1,0:T(4,128)} %param.7) | copy-start | bytes 196
  6.5 65.1 %reduce-scatter.2.cloned.1.call-start = ((), (), s32[]{:S(2)}) async-start(), calls=%async_computation.1 | async-start | bytes 1966080 | tf_op jit(solution)/shard_map/reduce_scatter | solution.py:107
  7.5 11.1 %collective-permute-start = (bf16[128,4,256]{2,0,1:T(8,128)(2,1)S(1)}, bf16[128,4,256]{2,0,1:T(8,128)(2,1)S(1)}, u32[]{:S(2)}, u32[]{:S(2)}) collective-permute-start(bf16[128,4,256]{2,0,1:T(8,128)(2,1)S(1)} %bitcast.69), channel_id=1, source_target_pairs={{0,2},{2,4},{4,6},{6,0},{1,3},{3,5},{5,7},{7,1},{8,10},{10,12},{12... | collective-permute-start | bytes 786440 | tf_op jit(solution)/shard_map/ppermute | solution.py:14
  10.6 14.3 %collective-permute-start.1 = (bf16[128,4,256]{2,0,1:T(8,128)(2,1)S(1)}, bf16[128,4,256]{2,0,1:T(8,128)(2,1)S(1)}, u32[]{:S(2)}, u32[]{:S(2)}) collective-permute-start(bf16[128,4,256]{2,0,1:T(8,128)(2,1)S(1)} %bitcast.70), channel_id=1, source_target_pairs={{0,6},{2,0},{4,2},{6,4},{1,7},{3,1},{5,3},{7,5},{8,14},{10,8},{12,... | collective-permute-start | bytes 786440 | tf_op jit(solution)/shard_map/ppermute | solution.py:17
  18.7 10.4 %collective-permute-start.2 = (bf16[128,4,256]{2,0,1:T(8,128)(2,1)S(1)}, bf16[128,4,256]{2,0,1:T(8,128)(2,1)S(1)}, u32[]{:S(2)}, u32[]{:S(2)}) collective-permute-start(bf16[128,4,256]{2,0,1:T(8,128)(2,1)S(1)} %collective-permute-done), channel_id=1, source_target_pairs={{0,2},{2,4},{4,6},{6,0},{1,3},{3,5},{5,7},{7,1},{8,10},{10,12},{12... | collective-permute-start | bytes 786440 | tf_op jit(solution)/shard_map/ppermute | solution.py:14
  33.1 17.0 %collective-permute-start.3 = (bf16[1,128,4,640]{3,1,2,0:T(8,128)(2,1)S(1)}, bf16[1,128,4,640]{3,1,2,0:T(8,128)(2,1)S(1)}, u32[]{:S(2)}, u32[]{:S(2)}) collective-permute-start(bf16[1,128,4,640]{3,1,2,0:T(8,128)(2,1)S(1)} %copy.21), channel_id=1, source_target_pairs={{0,24},{8,0},{16,8},{24,16},{1,25},{9,1},{17,9},{25,17},{2,26},{10... | collective-permute-start | bytes 1966088 | tf_op jit(solution)/shard_map/ppermute | solution.py:26
Sparse Core Ops, SparseCore 0:
  62.0 9.6 reduce-scatter.1
